TPU v7x, 32 devices: a whole 2x2x4 slice. The times are simulated.
32 devices in a mesh: groups: 2 (over y), clip: 4 (over z), strip: 4 (over x, core).
Axes of the slice: x: 2, y: 2, z: 4, core: 2. Of those that a mesh axis runs over, the one named last changes fastest.
Arguments:
- latents: bfloat16 [32, 20, 64, 320], P(('groups', 'clip'), 'strip'), parts along dimension 0, may hold values from -6 to 6
- anchor_index: int32 [8, 1], P(('groups', 'clip')), parts along dimension 0, may hold values from 0 to 3
- window: int32 [1], replicated, may hold values from 2 to 4
- gain_one: float32 [320], replicated, may hold values from 0.5 to 1.5
- spatial_w: bfloat16 [3, 3, 320, 320], replicated, may hold values from -0.109375 to 0.109375
- gain_two: float32 [320], replicated, may hold values from 0.5 to 1.5
- temporal_w: bfloat16 [3, 320, 320], replicated, may hold values from -0.1875 to 0.1875
- gain_three: float32 [320], replicated, may hold values from 0.5 to 1.5
- w_query: bfloat16 [320, 320], replicated
- w_keyval: bfloat16 [320, 640], replicated
- w_out: bfloat16 [320, 320], replicated, may hold values from -0.3125 to 0.3125
Outputs:
- block_out: bfloat16 [32, 20, 64, 320], P(('groups', 'clip'), 'strip'), parts along dimension 0
There are 2 independent parts, one for each index of `groups`. A program takes and returns all parts, laid end to end along the dimension named above; an argument that names none is the same for every part. Nothing has to cross between parts.
Inputs may be any that keep to these rules, and one draw needn't show every extreme that they name: `anchor_index`: indices of anchor frames within their clip of 4 frames. Frames closer than window[0] within one clip attend to each other.
All inputs are finite; a program needn't handle non-finite values.
Results may differ from a plain program's by a relative error of at most 0.0085.
Values may be sent and summed in bfloat16 or wider, within the bound.
A program may use at most 128 MiB of HBM per device.

v0:
```python
import functools
import math

import jax
import jax.numpy as jnp
from jax import lax
from jax.experimental import pallas as pl
from jax.experimental.pallas import tpu as pltpu
from jax.sharding import PartitionSpec as P

HEAD_DIM = 64
MESH = pl.DeviceIdType.MESH
F32 = jnp.float32
BF16 = jnp.bfloat16


def norm_rows(values, gain):
    inv = 1.0 / values.shape[0]
    centred = values - jnp.sum(values, axis=0, keepdims=True) * inv
    variance = jnp.sum(centred * centred, axis=0, keepdims=True) * inv
    return centred * lax.rsqrt(variance + 1e-05) * gain


def silu(u):
    return u / (1.0 + jnp.exp(-u))


def kernel(
    dims,
    latents, anchor_index, window, gain_one, spatial_w, gain_two, temporal_w, gain_three,
    w_query, w_keyval, w_out,
    out,
    lat, sw, tw, wq, wkv, wo, swt, twt, wqkvt, wot, gains,
    rim, taps, base, spatial, hidden, temporal, qkv, sent, clip_rim, anchors,
    local_sem, rim_send, rim_recv, clip_send, clip_recv, anchor_send, anchor_recv,
):
    frames, rows, columns, channels, strips, clips, picks = dims
    lanes = frames * columns
    half = channels // 2
    heads = channels // HEAD_DIM
    strip = lax.axis_index("strip")
    clip = lax.axis_index("clip")
    has_up, has_down = strip > 0, strip < strips - 1
    has_before, has_after = clip > 0, clip < clips - 1

    loads = [
        pltpu.make_async_copy(src, dst, local_sem.at[i])
        for i, (src, dst) in enumerate(
            ((latents, lat), (spatial_w, sw), (temporal_w, tw), (w_query, wq), (w_keyval, wkv), (w_out, wo))
        )
    ]
    for load in loads:
        load.start()

    barrier = pltpu.get_barrier_semaphore()

    @pl.when(has_up)
    def _():
        pl.semaphore_signal(barrier, inc=1, device_id={"strip": strip - 1}, device_id_type=MESH)

    @pl.when(has_down)
    def _():
        pl.semaphore_signal(barrier, inc=1, device_id={"strip": strip + 1}, device_id_type=MESH)

    others = [lax.rem(clip + d, clips) for d in range(1, clips)]
    for other in others:
        pl.semaphore_signal(barrier, inc=1, device_id={"clip": other}, device_id_type=MESH)
    pl.semaphore_wait(barrier, clips - 1 + has_up.astype(jnp.int32) + has_down.astype(jnp.int32))

    def rim_copy(side):
        source = latents.at[:, 0] if side == 1 else latents.at[:, rows - 1]
        return pltpu.make_async_remote_copy(
            src_ref=source, dst_ref=rim.at[side], send_sem=rim_send.at[side], recv_sem=rim_recv.at[side],
            device_id={"strip": strip - 1 if side == 1 else strip + 1}, device_id_type=MESH,
        )

    pl.when(has_up)(lambda: rim_copy(1).start())
    pl.when(has_down)(lambda: rim_copy(0).start())

    lane = lax.broadcasted_iota(jnp.int32, (1, lanes), 1)
    column = lax.rem(lane, columns)
    frame = lane // columns
    lane_half = lax.broadcasted_iota(jnp.int32, (1, 2 * columns), 1)
    low = lane_half < columns

    for i, ref in enumerate((gain_one, gain_two, gain_three)):
        gains[i] = jnp.broadcast_to(ref[...], (lanes, channels)).T

    def put_taps(slot, turned):
        wide = silu(norm_rows(turned, gains[0]))
        left = jnp.where(column == 0, 0.0, pltpu.roll(wide, 1, 1))
        right = jnp.where(column == columns - 1, 0.0, pltpu.roll(wide, lanes - 1, 1))
        taps[slot, 0:channels] = left.astype(BF16)
        taps[slot, channels : 2 * channels] = wide.astype(BF16)
        taps[slot, 2 * channels :] = right.astype(BF16)

    loads[0].wait()

    @pl.loop(0, rows)
    def _(r):
        turned = lat[:, r].reshape(lanes, channels).astype(F32).T
        base[r] = turned.astype(BF16)
        put_taps(r + 1, turned)

    loads[1].wait()
    for a in range(3):
        swt[a] = sw[a].reshape(3 * channels, channels).astype(F32).T.astype(BF16)
    for load in loads[2:]:
        load.wait()
    twt[...] = tw[...].reshape(3 * channels, channels).astype(F32).T.astype(BF16)
    wqkvt[0:channels] = wq[...].astype(F32).T.astype(BF16)
    wqkvt[channels:] = wkv[...].astype(F32).T.astype(BF16)
    wot[...] = wo[...].astype(F32).T.astype(BF16)

    def put_rim(side, slot, present):
        @pl.when(present)
        def _():
            rim_copy(side).wait_recv()
            put_taps(slot, rim[side].reshape(lanes, channels).astype(F32).T)

        @pl.when(jnp.logical_not(present))
        def _():
            taps[slot] = jnp.zeros(taps.shape[1:], BF16)

    def swap(values):
        return pltpu.roll(values, columns, 1)

    def clip_copy(side, r):
        return pltpu.make_async_remote_copy(
            src_ref=sent.at[side, r], dst_ref=clip_rim.at[side, r],
            send_sem=clip_send.at[side, r], recv_sem=clip_recv.at[side, r],
            device_id={"clip": clip - 1 if side == 1 else clip + 1}, device_id_type=MESH,
        )

    def convolve(r):
        total = base[r].astype(F32)
        for a in range(3):
            total = total + jnp.dot(swt[a], taps[r + a], preferred_element_type=F32)
        rounded = total.astype(BF16)
        spatial[r] = rounded
        wide = silu(norm_rows(rounded.astype(F32), gains[1])).astype(BF16)
        hidden[r] = wide
        wide = wide.astype(F32)
        first, last = wide[:, 0 : 2 * columns], wide[:, lanes - 2 * columns :]
        sent[1, r] = jnp.where(low, first[:half], swap(first[half:])).astype(BF16)
        sent[0, r] = jnp.where(low, swap(last[:half]), last[half:]).astype(BF16)
        pl.when(has_before)(lambda: clip_copy(1, r).start())
        pl.when(has_after)(lambda: clip_copy(0, r).start())

    def anchor_copy(slot, d, k, r, target):
        return pltpu.make_async_remote_copy(
            src_ref=anchors.at[slot, r], dst_ref=anchors.at[slot, r],
            send_sem=anchor_send.at[d * picks + k, r], recv_sem=anchor_recv.at[slot, r],
            device_id={"clip": target}, device_id_type=MESH,
        )

    def mix_frames(r):
        pl.when(has_before)(lambda: clip_copy(0, r).wait_recv())
        pl.when(has_after)(lambda: clip_copy(1, r).wait_recv())
        centre = hidden[r]
        wide = centre.astype(F32)
        before = clip_rim[0, r].astype(F32)
        after = clip_rim[1, r].astype(F32)
        before = jnp.where(has_before, jnp.concatenate([before, swap(before)], axis=0), 0.0)
        after = jnp.where(has_after, jnp.concatenate([swap(after), after], axis=0), 0.0)
        copies = lanes // (2 * columns)
        before = jnp.concatenate([before] * copies, axis=1)
        after = jnp.concatenate([after] * copies, axis=1)
        before = jnp.where(frame == 0, before, pltpu.roll(wide, columns, 1)).astype(BF16)
        after = jnp.where(frame == frames - 1, after, pltpu.roll(wide, lanes - columns, 1)).astype(BF16)
        stacked = jnp.concatenate([before, centre, after], axis=0)
        total = spatial[r].astype(F32) + jnp.dot(twt[...], stacked, preferred_element_type=F32)
        rounded = total.astype(BF16)
        temporal[r] = rounded
        normed = norm_rows(rounded.astype(F32), gains[2]).astype(BF16)
        wide = normed.astype(F32)
        for k in range(picks):
            pick = anchor_index[0, k]
            tile = wide[:, 0 : 2 * columns]
            for t in range(1, lanes // (2 * columns)):
                tile = jnp.where(pick >= 2 * t, wide[:, 2 * t * columns : 2 * (t + 1) * columns], tile)
            turned = swap(tile)
            odd = lax.rem(pick, 2) == 1
            upper = jnp.where(odd, turned[:half], tile[:half])
            lower = jnp.where(odd, tile[half:], turned[half:])
            slot = clip * picks + k
            anchors[slot, r] = jnp.where(low, upper, lower).astype(BF16)
            for d, other in enumerate(others):
                anchor_copy(slot, d, k, r, other).start()
        qkv[r] = jnp.dot(wqkvt[...], normed, preferred_element_type=F32).astype(BF16)

    def row_at(t):
        if rows < 3:
            return t
        return jnp.where(t < rows - 2, t + 1, jnp.where(t == rows - 2, 0, rows - 1))

    lag = 2

    @pl.loop(0, rows + lag)
    def _(t):
        @pl.when(t == max(rows - 2, 0))
        def _():
            put_rim(0, 0, has_up)
            put_rim(1, rows + 1, has_down)

        pl.when(t < rows)(lambda: convolve(row_at(t)))
        pl.when(t >= lag)(lambda: mix_frames(row_at(t - lag)))

    scale = 1.0 / math.sqrt(HEAD_DIM)
    groups = clips * picks // frames
    reach = window[0]

    def attend(r):
        for o in others:
            for k in range(picks):
                anchor_copy(o * picks + k, 0, k, r, o).wait_recv()
        keys = [qkv[r, channels : 2 * channels].astype(F32)]
        values = [qkv[r, 2 * channels :].astype(F32)]
        for g in range(groups):
            tiles = []
            for t in range(frames // 2):
                left = anchors[g * frames + 2 * t, r].astype(F32)
                right = anchors[g * frames + 2 * t + 1, r].astype(F32)
                upper = jnp.where(low, left, swap(right))
                lower = jnp.where(low, swap(left), right)
                tiles.append(jnp.concatenate([upper, lower], axis=0))
            normed = jnp.concatenate(tiles, axis=1).astype(BF16)
            both = jnp.dot(wqkvt[channels:], normed, preferred_element_type=F32).astype(BF16).astype(F32)
            keys.append(both[:channels])
            values.append(both[channels:])
        query = qkv[r, 0:channels].astype(F32)
        parts = []
        for h in range(heads):
            span = slice(h * HEAD_DIM, (h + 1) * HEAD_DIM)
            mine = query[span]
            scores = []
            for g, key in enumerate(keys):
                for step in range(frames):
                    moved = key[span]
                    if step:
                        moved = pltpu.roll(moved, lanes - step * columns, 1)
                    score = jnp.sum(mine * moved, axis=0, keepdims=True) * scale
                    if g == 0 and step:
                        away = jnp.abs(frame - lax.rem(frame + step, frames))
                        score = jnp.where(away < reach, score, -jnp.inf)
                    scores.append(score)
            top = functools.reduce(jnp.maximum, scores)
            weights = [jnp.exp(score - top) for score in scores]
            norm = functools.reduce(jnp.add, weights)
            mixed = jnp.zeros((HEAD_DIM, lanes), F32)
            for n, weight in enumerate(weights):
                prob = (weight / norm).astype(BF16).astype(F32)
                moved = values[n // frames][span]
                if n % frames:
                    moved = pltpu.roll(moved, lanes - (n % frames) * columns, 1)
                mixed = mixed + prob * moved
            parts.append(mixed.astype(BF16))
        attended = jnp.concatenate(parts, axis=0)
        total = temporal[r].astype(F32) + jnp.dot(wot[...], attended, preferred_element_type=F32)
        out[:, r] = total.T.reshape(frames, columns, channels).astype(out.dtype)

    @pl.loop(0, rows)
    def _(t):
        attend(row_at(t))

    pl.when(has_up)(lambda: rim_copy(1).wait_send())
    pl.when(has_down)(lambda: rim_copy(0).wait_send())

    @pl.loop(0, rows)
    def _(r):
        pl.when(has_before)(lambda: clip_copy(1, r).wait_send())
        pl.when(has_after)(lambda: clip_copy(0, r).wait_send())
        for d, other in enumerate(others):
            for k in range(picks):
                anchor_copy(clip * picks + k, d, k, r, other).wait_send()


def on_device(mesh, *args):
    latents, anchor_index = args[0], args[1]
    frames, rows, columns, channels = latents.shape
    strips, clips = mesh.shape["strip"], mesh.shape["clip"]
    picks = anchor_index.shape[1]
    lanes = frames * columns
    half = channels // 2
    assert frames % 2 == 0 and (clips * picks) % frames == 0
    dims = (frames, rows, columns, channels, strips, clips, picks)
    anywhere = pl.BlockSpec(memory_space=pl.ANY)
    vmem = pl.BlockSpec(memory_space=pltpu.VMEM)
    smem = pl.BlockSpec(memory_space=pltpu.SMEM)
    dma = pltpu.SemaphoreType.DMA
    args = [a.reshape(1, -1) if i in (3, 5, 7) else a for i, a in enumerate(args)]
    slots = clips * picks
    return pl.pallas_call(
        functools.partial(kernel, dims),
        out_shape=jax.ShapeDtypeStruct(latents.shape, latents.dtype),
        in_specs=[anywhere, smem, smem, vmem, anywhere, vmem, anywhere, vmem, anywhere, anywhere, anywhere],
        out_specs=vmem,
        scratch_shapes=[
            pltpu.VMEM(latents.shape, BF16),
            pltpu.VMEM(args[4].shape, BF16),
            pltpu.VMEM(args[6].shape, BF16),
            pltpu.VMEM(args[8].shape, BF16),
            pltpu.VMEM(args[9].shape, BF16),
            pltpu.VMEM(args[10].shape, BF16),
            pltpu.VMEM((3, channels, 3 * channels), BF16),
            pltpu.VMEM((channels, 3 * channels), BF16),
            pltpu.VMEM((3 * channels, channels), BF16),
            pltpu.VMEM((channels, channels), BF16),
            pltpu.VMEM((3, channels, lanes), F32),
            pltpu.VMEM((2, frames, columns, channels), BF16),
            pltpu.VMEM((rows + 2, 3 * channels, lanes), BF16),
            pltpu.VMEM((rows, channels, lanes), BF16),
            pltpu.VMEM((rows, channels, lanes), BF16),
            pltpu.VMEM((rows, channels, lanes), BF16),
            pltpu.VMEM((rows, channels, lanes), BF16),
            pltpu.VMEM((rows, 3 * channels, lanes), BF16),
            pltpu.VMEM((2, rows, half, 2 * columns), BF16),
            pltpu.VMEM((2, rows, half, 2 * columns), BF16),
            pltpu.VMEM((slots, rows, half, 2 * columns), BF16),
            dma((6,)),
            dma((2,)),
            dma((2,)),
            dma((2, rows)),
            dma((2, rows)),
            dma(((clips - 1) * picks, rows)),
            dma((slots, rows)),
        ],
        compiler_params=pltpu.CompilerParams(
            collective_id=0, has_side_effects=True, vmem_limit_bytes=60 * 2**20
        ),
        name="unet_block",
    )(*args)


def solution(mesh):
    return jax.shard_map(
        functools.partial(on_device, mesh),
        mesh=mesh,
        in_specs=(
            P(("groups", "clip"), "strip", None, None),
            P(("groups", "clip"), None),
            P(),
            P(),
            P(),
            P(),
            P(),
            P(),
            P(),
            P(),
            P(),
        ),
        out_specs=P(("groups", "clip"), "strip", None, None),
        check_vma=False,
    )
```

profile of v0, /device:TPU:0, one launch (start us, length us, event | category | flops | bytes accessed | tf_op | source)
XLA Modules:
  0.0 44.6 jit_solution(17685106548502703235)
XLA Ops:
  1.3 1.2 %reshape.9.gain_one = f32[1,320]{1,0:T(1,128)} reshape(f32[320]{0:T(512)} %param.14) | data formatting | bytes 2560 | tf_op jit(solution)/shard_map/reshape | solution.py:291
  2.5 1.3 %reshape.10.gain_two = f32[1,320]{1,0:T(1,128)} reshape(f32[320]{0:T(512)} %param.16) | data formatting | bytes 2560 | tf_op jit(solution)/shard_map/reshape | solution.py:291
  3.8 1.3 %reshape.11.gain_three = f32[1,320]{1,0:T(1,128)} reshape(f32[320]{0:T(512)} %param.18) | data formatting | bytes 2560 | tf_op jit(solution)/shard_map/reshape | solution.py:291
  5.1 37.3 %unet_block.1 = bf16[4,5,64,320]{3,2,1,0:T(8,128)(2,1)} custom-call(bf16[4,5,64,320]{3,2,1,0:T(8,128)(2,1)} %latents.1, s32[1,1]{1,0:T(1,128)S(6)} %copy.13.anchor_index, s32[1]{0:T(128)S(6)} %copy.14.window, f32[1,320]{1,0:T(1,128)} %reshape.9.gain_one, bf16[3,3,320,320]{3,2,1,0:T(8,128)(2,1)} %spatial_w.1, f32[1,320]{1,0:T(1,128)} %reshape.10.gain_two, ...), custom_call_target="tpu_custom_call" | custom-call | tf_op jit(solution)/shard_map/unet_block/pallas_call | solution.py:293
  42.4 2.2 %copy.15 = bf16[4,5,64,320]{3,2,1,0:T(8,128)(2,1)} copy(bf16[4,5,64,320]{3,2,1,0:T(8,128)(2,1)} %unet_block.1) | data formatting | bytes 1638400
where the time goes:
time: 44.9 us; the launch traced here: 44.6 us
  Pallas kernels  37.3 us (83%)
  local copies, waits for them, and re-layouts  6.02 us (13%)
  between operations  1.31 us (3%)
    pallas_call x1, Pallas kernels, on_device(): pl.pallas_call(functools.partial(kernel, dims), out_shape=jax.ShapeDtypeS...  37.3 us
    reshape x3, local copies, waits for them, and re-layouts, on_device(): a.reshape(1, -1)  3.77 us
    unnamed x1, local copies, waits for them, and re-layouts  2.25 us

commit v1 on v0

--- a/solution.py
+++ b/solution.py
@@ -32,7 +32,7 @@
     out,
     lat, sw, tw, wq, wkv, wo, swt, twt, wqkvt, wot, gains,
     rim, taps, base, spatial, hidden, temporal, qkv, sent, clip_rim, anchors,
-    local_sem, rim_send, rim_recv, clip_send, clip_recv, anchor_send, anchor_recv,
+    local_sem, rim_send, rim_recv, clip_send, clip_recv, anchor_send, anchor_recv, forward_send,
 ):
     frames, rows, columns, channels, strips, clips, picks = dims
     lanes = frames * columns
@@ -65,7 +65,6 @@
     others = [lax.rem(clip + d, clips) for d in range(1, clips)]
     for other in others:
         pl.semaphore_signal(barrier, inc=1, device_id={"clip": other}, device_id_type=MESH)
-    pl.semaphore_wait(barrier, clips - 1 + has_up.astype(jnp.int32) + has_down.astype(jnp.int32))
 
     def rim_copy(side):
         source = latents.at[:, 0] if side == 1 else latents.at[:, rows - 1]
@@ -74,9 +73,6 @@
             device_id={"strip": strip - 1 if side == 1 else strip + 1}, device_id_type=MESH,
         )
 
-    pl.when(has_up)(lambda: rim_copy(1).start())
-    pl.when(has_down)(lambda: rim_copy(0).start())
-
     lane = lax.broadcasted_iota(jnp.int32, (1, lanes), 1)
     column = lax.rem(lane, columns)
     frame = lane // columns
@@ -84,7 +80,8 @@
     low = lane_half < columns
 
     for i, ref in enumerate((gain_one, gain_two, gain_three)):
-        gains[i] = jnp.broadcast_to(ref[...], (lanes, channels)).T
+        turned = jnp.broadcast_to(ref[...].reshape(1, channels), (8, channels)).T
+        gains[i] = jnp.broadcast_to(turned[:, 0:1], (channels, lanes))
 
     def put_taps(slot, turned):
         wide = silu(norm_rows(turned, gains[0]))
@@ -94,23 +91,20 @@
         taps[slot, channels : 2 * channels] = wide.astype(BF16)
         taps[slot, 2 * channels :] = right.astype(BF16)
 
-    loads[0].wait()
-
-    @pl.loop(0, rows)
-    def _(r):
+    def prepare(r):
         turned = lat[:, r].reshape(lanes, channels).astype(F32).T
         base[r] = turned.astype(BF16)
         put_taps(r + 1, turned)
 
+    loads[0].wait()
+    pl.loop(0, 3)(prepare)
     loads[1].wait()
     for a in range(3):
         swt[a] = sw[a].reshape(3 * channels, channels).astype(F32).T.astype(BF16)
-    for load in loads[2:]:
-        load.wait()
-    twt[...] = tw[...].reshape(3 * channels, channels).astype(F32).T.astype(BF16)
-    wqkvt[0:channels] = wq[...].astype(F32).T.astype(BF16)
-    wqkvt[channels:] = wkv[...].astype(F32).T.astype(BF16)
-    wot[...] = wo[...].astype(F32).T.astype(BF16)
+
+    pl.semaphore_wait(barrier, clips - 1 + has_up.astype(jnp.int32) + has_down.astype(jnp.int32))
+    pl.when(has_up)(lambda: rim_copy(1).start())
+    pl.when(has_down)(lambda: rim_copy(0).start())
 
     def put_rim(side, slot, present):
         @pl.when(present)
@@ -144,6 +138,8 @@
         first, last = wide[:, 0 : 2 * columns], wide[:, lanes - 2 * columns :]
         sent[1, r] = jnp.where(low, first[:half], swap(first[half:])).astype(BF16)
         sent[0, r] = jnp.where(low, swap(last[:half]), last[half:]).astype(BF16)
+
+    def convolve_send(r):
         pl.when(has_before)(lambda: clip_copy(1, r).start())
         pl.when(has_after)(lambda: clip_copy(0, r).start())
 
@@ -154,9 +150,37 @@
             device_id={"clip": target}, device_id_type=MESH,
         )
 
-    def mix_frames(r):
+    def forward_copy(side, k, r):
+        slot = (clip + 1 if side == 1 else clip - 1) * picks + k
+        return pltpu.make_async_remote_copy(
+            src_ref=anchors.at[slot, r], dst_ref=anchors.at[slot, r],
+            send_sem=forward_send.at[side * picks + k, r], recv_sem=anchor_recv.at[slot, r],
+            device_id={"clip": clip - 1 if side == 1 else clip + 1}, device_id_type=MESH,
+        )
+
+    def forward(r):
+        for k in range(picks):
+            for side, near, far in ((0, has_before, has_after), (1, has_after, has_before)):
+
+                @pl.when(near)
+                def _():
+                    slot = (clip + 1 if side == 1 else clip - 1) * picks + k
+                    target = clip + 1 if side == 1 else clip - 1
+                    anchor_copy(slot, 0, k, r, target).wait_recv()
+
+                pl.when(jnp.logical_and(near, far))(lambda: forward_copy(side, k, r).start())
+
+    def mix_wait(r):
         pl.when(has_before)(lambda: clip_copy(0, r).wait_recv())
         pl.when(has_after)(lambda: clip_copy(1, r).wait_recv())
+
+    def mix_send(r):
+        for k in range(picks):
+            for d, other in enumerate(others):
+                direct = jnp.abs(other - clip) != 2
+                pl.when(direct)(lambda: anchor_copy(clip * picks + k, d, k, r, other).start())
+
+    def mix_frames(r):
         centre = hidden[r]
         wide = centre.astype(F32)
         before = clip_rim[0, r].astype(F32)
@@ -185,26 +209,44 @@
             lower = jnp.where(odd, tile[half:], turned[half:])
             slot = clip * picks + k
             anchors[slot, r] = jnp.where(low, upper, lower).astype(BF16)
-            for d, other in enumerate(others):
-                anchor_copy(slot, d, k, r, other).start()
         qkv[r] = jnp.dot(wqkvt[...], normed, preferred_element_type=F32).astype(BF16)
 
     def row_at(t):
-        if rows < 3:
-            return t
         return jnp.where(t < rows - 2, t + 1, jnp.where(t == rows - 2, 0, rows - 1))
 
     lag = 2
-
-    @pl.loop(0, rows + lag)
+    convolve(1)
+    convolve_send(1)
+    for load in loads[2:]:
+        load.wait()
+    twt[...] = tw[...].reshape(3 * channels, channels).astype(F32).T.astype(BF16)
+    pl.loop(3, rows)(prepare)
+    convolve(row_at(1))
+    convolve_send(row_at(1))
+    wqkvt[0:channels] = wq[...].astype(F32).T.astype(BF16)
+    wqkvt[channels:] = wkv[...].astype(F32).T.astype(BF16)
+    wot[...] = wo[...].astype(F32).T.astype(BF16)
+
+    @pl.loop(lag, rows)
     def _(t):
-        @pl.when(t == max(rows - 2, 0))
+        @pl.when(t == rows - 2)
         def _():
             put_rim(0, 0, has_up)
             put_rim(1, rows + 1, has_down)
 
-        pl.when(t < rows)(lambda: convolve(row_at(t)))
-        pl.when(t >= lag)(lambda: mix_frames(row_at(t - lag)))
+        mix_wait(row_at(t - lag))
+        mix_frames(row_at(t - lag))
+        convolve(row_at(t))
+        mix_send(row_at(t - lag))
+        convolve_send(row_at(t))
+        pl.when(t > lag)(lambda: forward(row_at(t - lag - 1)))
+
+    @pl.loop(rows, rows + lag)
+    def _(t):
+        mix_wait(row_at(t - lag))
+        mix_frames(row_at(t - lag))
+        mix_send(row_at(t - lag))
+        forward(row_at(t - lag - 1))
 
     scale = 1.0 / math.sqrt(HEAD_DIM)
     groups = clips * picks // frames
@@ -213,7 +255,8 @@
     def attend(r):
         for o in others:
             for k in range(picks):
-                anchor_copy(o * picks + k, 0, k, r, o).wait_recv()
+                distant = jnp.abs(o - clip) > 1
+                pl.when(distant)(lambda: anchor_copy(o * picks + k, 0, k, r, o).wait_recv())
         keys = [qkv[r, channels : 2 * channels].astype(F32)]
         values = [qkv[r, 2 * channels :].astype(F32)]
         for g in range(groups):
@@ -262,6 +305,7 @@
     @pl.loop(0, rows)
     def _(t):
         attend(row_at(t))
+        pl.when(t == 0)(lambda: forward(row_at(rows - 1)))
 
     pl.when(has_up)(lambda: rim_copy(1).wait_send())
     pl.when(has_down)(lambda: rim_copy(0).wait_send())
@@ -272,7 +316,12 @@
         pl.when(has_after)(lambda: clip_copy(0, r).wait_send())
         for d, other in enumerate(others):
             for k in range(picks):
-                anchor_copy(clip * picks + k, d, k, r, other).wait_send()
+                direct = jnp.abs(other - clip) != 2
+                pl.when(direct)(lambda: anchor_copy(clip * picks + k, d, k, r, other).wait_send())
+        for k in range(picks):
+            for side in range(2):
+                both = jnp.logical_and(has_before, has_after)
+                pl.when(both)(lambda: forward_copy(side, k, r).wait_send())
 
 
 def on_device(mesh, *args):
@@ -282,13 +331,12 @@
     picks = anchor_index.shape[1]
     lanes = frames * columns
     half = channels // 2
-    assert frames % 2 == 0 and (clips * picks) % frames == 0
+    assert rows >= 4 and frames % 2 == 0 and (clips * picks) % frames == 0
     dims = (frames, rows, columns, channels, strips, clips, picks)
     anywhere = pl.BlockSpec(memory_space=pl.ANY)
     vmem = pl.BlockSpec(memory_space=pltpu.VMEM)
     smem = pl.BlockSpec(memory_space=pltpu.SMEM)
     dma = pltpu.SemaphoreType.DMA
-    args = [a.reshape(1, -1) if i in (3, 5, 7) else a for i, a in enumerate(args)]
     slots = clips * picks
     return pl.pallas_call(
         functools.partial(kernel, dims),
@@ -324,9 +372,10 @@
             dma((2, rows)),
             dma(((clips - 1) * picks, rows)),
             dma((slots, rows)),
+            dma((2 * picks, rows)),
         ],
         compiler_params=pltpu.CompilerParams(
-            collective_id=0, has_side_effects=True, vmem_limit_bytes=60 * 2**20
+            collective_id=0, has_side_effects=True, vmem_limit_bytes=56 * 2**20
         ),
         name="unet_block",
     )(*args)

time: 44.9 us -> 39.2 us (0.87)
  local copies, waits for them, and re-layouts: 6.02 us -> 2.25 us
  Pallas kernels: 37.3 us -> 35.5 us
    reshape x3 -> x0, local copies, waits for them, and re-layouts: 3.77 us -> none  [on_device(): a.reshape(1, -1)]
    pallas_call x1, Pallas kernels: 37.3 us -> 35.5 us  [on_device(): pl.pallas_call(functools.partial(kernel, dims), out_shape=jax.ShapeDtypeS...]
where the time goes in v1:
time: 39.2 us; the launch traced here: 39 us
  Pallas kernels  35.5 us (91%)
  local copies, waits for them, and re-layouts  2.25 us (6%)
  between operations  1.3 us (3%)
    pallas_call x1, Pallas kernels, on_device(): pl.pallas_call(functools.partial(kernel, dims), out_shape=jax.ShapeDtypeS...  35.5 us
    unnamed x1, local copies, waits for them, and re-layouts  2.25 us

profile of v1, /device:TPU:0, one launch (start us, length us, event | category | flops | bytes accessed | tf_op | source)
XLA Modules:
  0.0 39.0 jit_solution(13752273770920521328)
XLA Ops:
  1.3 35.5 %unet_block.1 = bf16[4,5,64,320]{3,2,1,0:T(8,128)(2,1)} custom-call(bf16[4,5,64,320]{3,2,1,0:T(8,128)(2,1)} %latents.1, s32[1,1]{1,0:T(1,128)S(6)} %copy.13.anchor_index, s32[1]{0:T(128)S(6)} %copy.14.window, f32[320]{0:T(512)} %gain_one.1, bf16[3,3,320,320]{3,2,1,0:T(8,128)(2,1)} %spatial_w.1, f32[320]{0:T(512)} %gain_two.1, ...), custom_call_target="tpu_custom_call" | custom-call | tf_op jit(solution)/shard_map/unet_block/pallas_call | solution.py:341
  36.8 2.2 %copy.15 = bf16[4,5,64,320]{3,2,1,0:T(8,128)(2,1)} copy(bf16[4,5,64,320]{3,2,1,0:T(8,128)(2,1)} %unet_block.1) | data formatting | bytes 1638400

commit v2 on v1

--- a/solution.py
+++ b/solution.py
@@ -214,7 +214,8 @@
     def row_at(t):
         return jnp.where(t < rows - 2, t + 1, jnp.where(t == rows - 2, 0, rows - 1))
 
-    lag = 2
+    lag = 3
+    delay = 2
     convolve(1)
     convolve_send(1)
     for load in loads[2:]:
@@ -226,6 +227,9 @@
     wqkvt[0:channels] = wq[...].astype(F32).T.astype(BF16)
     wqkvt[channels:] = wkv[...].astype(F32).T.astype(BF16)
     wot[...] = wo[...].astype(F32).T.astype(BF16)
+    for t in range(2, lag):
+        convolve(row_at(t))
+        convolve_send(row_at(t))
 
     @pl.loop(lag, rows)
     def _(t):
@@ -236,17 +240,17 @@
 
         mix_wait(row_at(t - lag))
         mix_frames(row_at(t - lag))
+        mix_send(row_at(t - lag))
         convolve(row_at(t))
-        mix_send(row_at(t - lag))
         convolve_send(row_at(t))
-        pl.when(t > lag)(lambda: forward(row_at(t - lag - 1)))
+        pl.when(t >= lag + delay)(lambda: forward(row_at(t - lag - delay)))
 
     @pl.loop(rows, rows + lag)
     def _(t):
         mix_wait(row_at(t - lag))
         mix_frames(row_at(t - lag))
         mix_send(row_at(t - lag))
-        forward(row_at(t - lag - 1))
+        pl.when(t >= lag + delay)(lambda: forward(row_at(t - lag - delay)))
 
     scale = 1.0 / math.sqrt(HEAD_DIM)
     groups = clips * picks // frames
@@ -305,7 +309,7 @@
     @pl.loop(0, rows)
     def _(t):
         attend(row_at(t))
-        pl.when(t == 0)(lambda: forward(row_at(rows - 1)))
+        pl.when(t < delay)(lambda: forward(row_at(t + rows - delay)))
 
     pl.when(has_up)(lambda: rim_copy(1).wait_send())
     pl.when(has_down)(lambda: rim_copy(0).wait_send())

time: 39.2 us -> 37.9 us (0.967)
  Pallas kernels: 35.5 us -> 34.2 us
    pallas_call x1, Pallas kernels: 35.5 us -> 34.2 us  [on_device(): pl.pallas_call(functools.partial(kernel, dims), out_shape=jax.ShapeDtypeS...]
where the time goes in v2:
time: 37.9 us; the launch traced here: 37.7 us
  Pallas kernels  34.2 us (90%)
  local copies, waits for them, and re-layouts  2.25 us (6%)
  between operations  1.3 us (3%)
    pallas_call x1, Pallas kernels, on_device(): pl.pallas_call(functools.partial(kernel, dims), out_shape=jax.ShapeDtypeS...  34.2 us
    unnamed x1, local copies, waits for them, and re-layouts  2.25 us

profile of v2, /device:TPU:0, one launch (start us, length us, event | category | flops | bytes accessed | tf_op | source)
XLA Modules:
  0.0 37.7 jit_solution(8720847449654091056)
XLA Ops:
  1.3 34.2 %unet_block.1 = bf16[4,5,64,320]{3,2,1,0:T(8,128)(2,1)} custom-call(bf16[4,5,64,320]{3,2,1,0:T(8,128)(2,1)} %latents.1, s32[1,1]{1,0:T(1,128)S(6)} %copy.13.anchor_index, s32[1]{0:T(128)S(6)} %copy.14.window, f32[320]{0:T(512)} %gain_one.1, bf16[3,3,320,320]{3,2,1,0:T(8,128)(2,1)} %spatial_w.1, f32[320]{0:T(512)} %gain_two.1, ...), custom_call_target="tpu_custom_call" | custom-call | tf_op jit(solution)/shard_map/unet_block/pallas_call | solution.py:345
  35.5 2.2 %copy.15 = bf16[4,5,64,320]{3,2,1,0:T(8,128)(2,1)} copy(bf16[4,5,64,320]{3,2,1,0:T(8,128)(2,1)} %unet_block.1) | data formatting | bytes 1638400
